TPU v7x, 256 devices: a whole 4x4x8 slice. The times are simulated.
256 devices in a mesh: row: 128 (over z, y_lo, x, core), ch: 2 (over y_hi).
Axes of the slice: x: 4, y: 4 (y_hi: 2, y_lo: 2; y = y_hi * 2 + y_lo), z: 8, core: 2. Of those that a mesh axis runs over, the one named last changes fastest.
Arguments:
- pair_rep: bfloat16 [384, 384, 128], P('row'), may hold values from -6 to 6
- res_mask: int32 [384], replicated, may hold values 0 or 1
- in_gain: float32 [128], replicated, may hold values from 0.5 to 1.5
- w_left: bfloat16 [128, 128], P(None, 'ch'), may hold values from -0.5 to 0.5
- w_left_gate: bfloat16 [128, 128], P(None, 'ch'), may hold values from -0.5 to 0.5
- w_right: bfloat16 [128, 128], P(None, 'ch'), may hold values from -0.5 to 0.5
- w_right_gate: bfloat16 [128, 128], P(None, 'ch'), may hold values from -0.5 to 0.5
- w_gate: bfloat16 [128, 128], replicated, may hold values from -0.5 to 0.5
- mid_gain: float32 [128], replicated, may hold values from 0.5 to 1.5
- w_out: bfloat16 [128, 128], replicated, may hold values from -0.5 to 0.5
- next_gain: float32 [128], replicated, may hold values from 0.5 to 1.5
Outputs:
- new_pair: bfloat16 [384, 384, 128], P(None, 'row', 'ch')
- new_norm: bfloat16 [384, 384, 128], P(None, 'row', 'ch')
All inputs are finite; a program needn't handle non-finite values.
Results may differ from a plain program's by a relative error of at most 0.0065.
Values may be sent and summed in bfloat16 or wider, within the bound.
A program may use at most 64 MiB of HBM per device.

v0:
```python
import jax
import jax.numpy as jnp
from jax import lax
from jax.sharding import Mesh
from jax.sharding import PartitionSpec as P

ROW = ("row_0", "row_1", "row_2", "row_3")
epsilon = 1e-05


def split_up(array, dim, devices):
    dims = array.shape
    blocks = array.reshape(*dims[:dim], devices, dims[dim] // devices, *dims[dim + 1 :])
    return jnp.moveaxis(blocks, dim, 0)


def in_order(blocks, dim):
    dims = list(blocks.shape[1:])
    dims[dim] *= blocks.shape[0]
    return jnp.moveaxis(blocks, 0, dim).reshape(dims)


def moved_by_axis(blocks, axes, order):
    inside = blocks.shape[1:]
    whole = blocks.reshape(*(lax.axis_size(a) for a in axes), *inside)
    for k in order:
        whole = lax.all_to_all(whole, axes[k], k, k, tiled=True)
    return whole.reshape(-1, *inside)


def exchange_by_chip(array, groups, order, split_dim, concat_dim):
    devices = lax.axis_size(groups[0]) * lax.axis_size(groups[1])
    blocks = split_up(array, split_dim, devices)
    return in_order(moved_by_axis(blocks, groups, order), concat_dim)


def copy_for_each(array, axis):
    copies = jnp.broadcast_to(array, (lax.axis_size(axis), *array.shape))
    return lax.all_to_all(copies, axis, split_axis=0, concat_axis=0, tiled=True)


def over_copies(array, axis):
    return copy_for_each(array, axis).sum(axis=0)


def together(arrays, axis):
    vector, at, gathered = (jnp.concatenate([a.reshape(-1) for a in arrays]), 0, [])
    so_far = over_copies(vector, axis)
    for a in arrays:
        gathered.append(so_far[at : at + a.size].reshape(a.shape))
        at += a.size
    return tuple(gathered)


def sum_at_owner(array, axis, dim):
    blocks = split_up(array, dim, lax.axis_size(axis))
    arrived = lax.all_to_all(blocks, axis, split_axis=0, concat_axis=0, tiled=True)
    return arrived.astype(jnp.float32).sum(axis=0)


def packed_total(arrays, axis):
    vector, at, gathered = (jnp.concatenate([a.reshape(-1) for a in arrays]), 0, [])
    so_far = lax.psum(vector, axis)
    for a in arrays:
        gathered.append(so_far[at : at + a.size].reshape(a.shape))
        at += a.size
    return tuple(gathered)


def normalize(values, scale_gain, along):
    values = values.astype(jnp.float32)
    average = jnp.mean(values, along, keepdims=True)
    centred = values - average
    spread = jnp.mean(centred * centred, along, keepdims=True)
    return centred * lax.rsqrt(spread + epsilon) * scale_gain


def gated(normed, weight, weight_gate, pair_mask):
    values_lin = jnp.einsum("ilc,ch->hil", normed, weight, preferred_element_type=jnp.float32)
    switch = jnp.einsum("ilc,ch->hil", normed, weight_gate, preferred_element_type=jnp.float32)
    return (jax.nn.sigmoid(switch) * values_lin * pair_mask[None]).astype(jnp.bfloat16)


def batched_rows(first, second):
    return lax.dot_general(
        first, second, (((2,), (2,)), ((0,), (0,))), preferred_element_type=jnp.float32
    )


def local(
    pair_rep,
    res_mask,
    in_gain,
    w_left,
    w_left_gate,
    w_right,
    w_right_gate,
    w_gate,
    mid_gain,
    w_out,
    next_gain,
):
    row_count = pair_rep.shape[0]
    channels = pair_rep.shape[2]
    hid_local = w_left.shape[1]
    ch_count = lax.axis_size("ch")
    ch_index = lax.axis_index("ch")
    row_index = lax.axis_index(ROW)
    ch_width = channels // ch_count
    res_float = res_mask.astype(jnp.float32)
    own_mask = lax.dynamic_slice_in_dim(res_float, row_index * row_count, row_count)
    pair_mask = own_mask[:, None] * res_float[None, :]
    normed = normalize(pair_rep, in_gain, 2).astype(jnp.bfloat16)
    left_side = gated(normed, w_left, w_left_gate, pair_mask)
    right_side = gated(normed, w_right, w_right_gate, pair_mask)
    pair_here = exchange_by_chip(pair_rep, (("row_0", "row_1", "row_2"), "row_3"), (1, 0), 1, 0)
    normed_here = normalize(pair_here, in_gain, 2).astype(jnp.bfloat16)
    triangle = batched_rows(right_side, lax.all_gather(left_side, ROW, axis=1, tiled=True))
    einsum_form = "kba,kc->abc"
    hidden_total = hid_local * ch_count
    stat_sums = together((jnp.sum(triangle, 0), jnp.sum(triangle * triangle, 0)), "ch")
    mean_vals = stat_sums[0] / hidden_total
    var_vals = stat_sums[1] / hidden_total - mean_vals * mean_vals
    own_gain = lax.dynamic_slice_in_dim(mid_gain, ch_index * hid_local, hid_local)
    tri_normed = (
        (triangle - mean_vals) * lax.rsqrt(var_vals + epsilon) * own_gain[:, None, None]
    ).astype(jnp.bfloat16)
    w_rows = lax.dynamic_slice_in_dim(w_out, ch_index * hid_local, hid_local, 0)
    partial_terms = jnp.einsum(einsum_form, tri_normed, w_rows, preferred_element_type=jnp.float32)
    update = sum_at_owner(partial_terms.astype(jnp.bfloat16), "ch", 2)
    w_cols = lax.dynamic_slice_in_dim(w_gate, ch_index * ch_width, ch_width, 1)
    gate_vals = jax.nn.sigmoid(
        jnp.einsum("abc,cd->abd", normed_here, w_cols, preferred_element_type=jnp.float32)
    )
    pair_half = lax.dynamic_slice_in_dim(pair_here, ch_index * ch_width, ch_width, 2)
    new_half = (pair_half.astype(jnp.float32) + gate_vals * update).astype(jnp.bfloat16)
    values = new_half.astype(jnp.float32)
    next_sums = packed_total((jnp.sum(values, 2), jnp.sum(values * values, 2)), "ch")
    next_mean = next_sums[0] / channels
    next_var = next_sums[1] / channels - next_mean * next_mean
    own_next = lax.dynamic_slice_in_dim(next_gain, ch_index * ch_width, ch_width)
    norm_half = (
        (values - next_mean[..., None]) * lax.rsqrt(next_var + epsilon)[..., None] * own_next
    ).astype(jnp.bfloat16)
    return (new_half, norm_half)


def solution(mesh):
    split = Mesh(
        mesh.devices.reshape(8, 2, 4, 2, mesh.shape["ch"]),
        ("row_0", "row_1", "row_2", "row_3", "ch"),
    )
    return jax.shard_map(
        local,
        mesh=split,
        in_specs=(
            P(ROW, None, None),
            P(),
            P(),
            P(None, "ch"),
            P(None, "ch"),
            P(None, "ch"),
            P(None, "ch"),
            P(),
            P(),
            P(),
            P(),
        ),
        out_specs=(P(None, ROW, "ch"), P(None, ROW, "ch")),
        check_vma=False,
    )
```

profile of v0, /device:TPU:16, one launch (start us, length us, event | category | flops | bytes accessed | tf_op | source)
XLA Modules:
  0.0 321.3 jit_solution(7978292074478839061)
XLA Ops:
  7.2 0.0 copy-start
  7.2 0.0 all-gather.2.cloned.1.call-start
  7.2 0.7 convert_element_type.55
  7.9 0.1 dynamic_slice.21
  8.0 0.1 broadcast_multiply_fusion.1
  8.1 1.1 convert_reduce_fusion
  9.2 1.4 fusion.22
  10.6 1.5 fusion.6
  12.1 0.0 copy-start.2
  12.1 0.0 copy-start.3
  12.2 2.2 fusion.18
  14.3 0.0 all-gather.2.cloned.1.call-update
  14.4 1.3 reshape.148
  15.7 0.1 copy.83
  15.8 4.0 %all_to_all.21 = bf16[64,2,3,3,128]{4,0,3,2,1:T(8,128)(2,1)S(1)} all-to-all(bf16[64,2,3,3,128]{4,0,3,2,1:T(8,128)(2,1)S(1)} %copy.83), channel_id=1, replica_groups=mesh['row_0'=8,'row_1'=2,'row_2'=4,'row_3'=2,'ch'=2] {'row_3'}, dimensions={1} | all-to-all | bytes 589824 | tf_op jit(solution)/shard_map/all_to_all | solution.py:27
  19.7 1.0 copy.84
  20.7 12.7 %all-to-all-start.1 = ((bf16[64,2,3,3,128]{4,1,3,2,0:T(2,128)(2,1)}), bf16[64,2,3,3,128]{4,1,3,2,0:T(2,128)(2,1)S(1)}, u32[]{:S(2)}, u32[]{:S(2)}) async-start(bf16[64,2,3,3,128]{4,1,3,2,0:T(2,128)(2,1)} %copy.84), calls=%async_computation.1 | async-start | bytes 589824 | tf_op jit(solution)/shard_map/all_to_all | solution.py:27
  33.4 0.7 dynamic_slice.22
  34.1 0.7 dynamic_slice.23
  34.9 1.5 fusion.9
  36.4 1.5 fusion.19
  37.9 10.0 %all-to-all-done.1 = bf16[64,2,3,3,128]{4,1,3,2,0:T(2,128)(2,1)S(1)} async-done(((bf16[64,2,3,3,128]{4,1,3,2,0:T(2,128)(2,1)}), bf16[64,2,3,3,128]{4,1,3,2,0:T(2,128)(2,1)S(1)}, u32[]{:S(2)}, u32[]{:S(2)}) %all-to-all-start.1) | async-done | bytes 294944 | tf_op jit(solution)/shard_map/all_to_all | solution.py:27
  48.0 0.2 copy.85
  48.2 0.2 reshape_reshape.3
  48.4 0.9 convert_reduce_fusion.1
  49.3 0.1 broadcast_multiply_fusion
  49.3 1.7 fusion.26
  51.1 200.2 %all-gather.2.cloned.1.call-done = bf16[64,384,384]{2,0,1:T(8,128)(2,1)} async-done(((bf16[64,3,384]{2,0,1:T(8,128)(2,1)}), bf16[64,384,384]{2,0,1:T(8,128)(2,1)}) %all-gather.2.cloned.1.call-update) | async-done | bytes 18874384 | tf_op jit(solution)/shard_map/all_gather | solution.py:118
  251.3 29.4 %fusion.50 = (f32[3,384]{1,0:T(4,128)S(1)}, f32[3,384]{1,0:T(4,128)S(1)}, f32[64,3,384]{2,1,0:T(4,128)S(1)}) fusion(bf16[64,384,384]{2,0,1:T(8,128)(2,1)} %all-gather.2.cloned.1.call-done, bf16[64,3,384]{2,0,1:T(8,128)(2,1)S(1)} %fusion.19), kind=kOutput, calls=%fused_computation.78 | convolution fusion | flops 56841984 | bytes 19325952 | tf_op jit(solution)/shard_map/dot_general | solution.py:85
  280.7 0.3 pad_maximum_fusion
  281.0 0.6 broadcast_in_dim.2
  281.6 5.0 %all-to-all-start.2 = ((f32[2,1,2304]{2,1,0:T(1,128)}), f32[2,1,2304]{2,1,0:T(1,128)S(1)}, u32[]{:S(2)}, u32[]{:S(2)}) async-start(f32[2,1,2304]{2,1,0:T(1,128)} %broadcast_in_dim.2), calls=%async_computation.2 | async-start | bytes 36864 | tf_op jit(solution)/shard_map/all_to_all | solution.py:39
  286.6 0.1 constant_dynamic-slice_fusion
  286.8 1.3 copy.88
  288.0 0.2 copy.105
  288.2 0.2 all-to-all-done.2
  288.5 0.1 multiply_convert_fusion.1
  288.7 0.0 copy-done
  288.7 0.3 convolution_convert_fusion
  289.0 0.7 copy.124
  289.7 7.0 %all-to-all-start.3 = ((bf16[2,384,3,64]{1,3,2,0:T(8,128)(2,1)}), bf16[2,384,3,64]{1,3,2,0:T(8,128)(2,1)S(1)}, u32[]{:S(2)}, u32[]{:S(2)}) async-start(bf16[2,384,3,64]{1,3,2,0:T(8,128)(2,1)} %bitcast.39), calls=%async_computation.3 | async-start | bytes 589824 | tf_op jit(solution)/shard_map/all_to_all | solution.py:57
  296.7 0.1 add_rsqrt_fusion
  296.8 1.3 copy.91
  298.1 0.3 rsqrt.26
  298.4 0.3 div.50
  298.6 1.4 all-to-all-done.3
  300.1 0.0 copy-done.2
  300.1 0.0 copy-done.3
  300.1 0.6 convert_reduce_fusion.3
  300.7 0.0 copy-start.1
  300.7 0.1 copy.98
  300.8 0.2 reshape.153
  301.1 0.1 copy.99
  301.2 0.2 reshape.154
  301.4 11.6 %psum.7 = f32[2304]{0:T(1024)S(1)} all-reduce(f32[2304]{0:T(1024)S(1)} %pad_maximum_fusion.1), channel_id=1, replica_groups=mesh['row_0'=8,'row_1'=2,'row_2'=4,'row_3'=2,'ch'=2] {'ch'}, use_global_device_ids=true, to_apply=%region_10.0 | all-reduce | flops 2304 | bytes 18432 | tf_op jit(solution)/shard_map/psum | solution.py:63
  313.1 0.2 div.64
  313.3 0.1 copy.100
  313.3 0.2 div.66
  313.6 0.1 copy.103
  313.7 0.8 fusion.30
  314.5 0.0 copy-done.1
  (13 shorter events, 0.2 us)
Async XLA Ops:
  7.2 281.5 %copy-start = (bf16[128,128]{1,0:T(8,128)(2,1)S(1)}, bf16[128,128]{1,0:T(8,128)(2,1)}, u32[]{:S(2)}) copy-start(bf16[128,128]{1,0:T(8,128)(2,1)} %param.20) | copy-start | bytes 98308
  7.2 244.2 %all-gather.2.cloned.1.call-start = ((), (), s32[]{:S(2)}) async-start(), calls=%async_computation.4 | async-start | bytes 19021824 | tf_op jit(solution)/shard_map/all_gather | solution.py:118
  12.1 287.9 %copy-start.2 = (bf16[128,128]{1,0:T(8,128)(2,1)S(1)}, bf16[128,128]{1,0:T(8,128)(2,1)}, u32[]{:S(2)}) copy-start(bf16[128,128]{1,0:T(8,128)(2,1)} %param.18) | copy-start | bytes 98308
  12.1 287.9 %copy-start.3 = (f32[128]{0:T(128)S(1)}, f32[128]{0:T(128)}, u32[]{:S(2)}) copy-start(f32[128]{0:T(128)} %param.13) | copy-start | bytes 1540
  20.7 27.2 %all-to-all-start.1 = ((bf16[64,2,3,3,128]{4,1,3,2,0:T(2,128)(2,1)}), bf16[64,2,3,3,128]{4,1,3,2,0:T(2,128)(2,1)S(1)}, u32[]{:S(2)}, u32[]{:S(2)}) async-start(bf16[64,2,3,3,128]{4,1,3,2,0:T(2,128)(2,1)} %copy.84), calls=%async_computation.1 | async-start | bytes 589824 | tf_op jit(solution)/shard_map/all_to_all | solution.py:27
  281.6 6.8 %all-to-all-start.2 = ((f32[2,1,2304]{2,1,0:T(1,128)}), f32[2,1,2304]{2,1,0:T(1,128)S(1)}, u32[]{:S(2)}, u32[]{:S(2)}) async-start(f32[2,1,2304]{2,1,0:T(1,128)} %broadcast_in_dim.2), calls=%async_computation.2 | async-start | bytes 36864 | tf_op jit(solution)/shard_map/all_to_all | solution.py:39
  289.7 10.3 %all-to-all-start.3 = ((bf16[2,384,3,64]{1,3,2,0:T(8,128)(2,1)}), bf16[2,384,3,64]{1,3,2,0:T(8,128)(2,1)S(1)}, u32[]{:S(2)}, u32[]{:S(2)}) async-start(bf16[2,384,3,64]{1,3,2,0:T(8,128)(2,1)} %bitcast.39), calls=%async_computation.3 | async-start | bytes 589824 | tf_op jit(solution)/shard_map/all_to_all | solution.py:57
  300.7 13.8 %copy-start.1 = (bf16[384,3,64]{0,2,1:T(8,128)(2,1)}, bf16[384,3,64]{0,2,1:T(8,128)(2,1)S(1)}, u32[]{:S(2)}) copy-start(bf16[384,3,64]{0,2,1:T(8,128)(2,1)S(1)} %get-tuple-element.11) | copy-start | bytes 442372
Sparse Core Ops, SparseCore 0:
  14.5 236.8 all-gather.1
where the time goes:
time: 322 us; the launch traced here: 321 us
  waiting for transfers between devices  212 us (66%)
  matrix products  37 us (11%)
  starting transfers between devices  24.6 us (8%)
  blocking collectives  15.6 us (5%)
  between operations  14.3 us (4%)
  local copies, waits for them, and re-layouts  10.5 us (3%)
  other arithmetic  7.41 us (2%)
    all_gather x1, waiting for transfers between devices, local(): lax.all_gather(left_side, ROW, axis=1, tiled=True)  200 us
    dot_general x1, matrix products, batched_rows(): lax.dot_general(first, second, (((2,), (2,)), ((0,), (0,))), preferred_el...  29.4 us
    all_to_all x1, starting transfers between devices, moved_by_axis(): whole = lax.all_to_all(whole, axes[k], k, k, tiled=True)  12.7 us
    psum x1, blocking collectives, packed_total(): so_far = lax.psum(vector, axis)  11.6 us
    all_to_all x1, waiting for transfers between devices, moved_by_axis(): whole = lax.all_to_all(whole, axes[k], k, k, tiled=True)  10 us
    all_to_all x1, starting transfers between devices, sum_at_owner(): lax.all_to_all(blocks, axis, split_axis=0, concat_axis=0, tiled=True)  6.96 us
  transfers between devices with their start and end apart: 4, of which 4 were waited for; matrix products, arithmetic and copies ran while one was open for 4% of the time, Pallas kernels for 0%

commit v1 on v0

--- a/solution.py
+++ b/solution.py
@@ -6,6 +6,15 @@
 
 ROW = ("row_0", "row_1", "row_2", "row_3")
 epsilon = 1e-05
+trace_joints = lambda block_in, bus_axis: jnp.concatenate(
+    lax.all_to_all(
+        jnp.stack([block_in] * lax.axis_size(bus_axis)),
+        axis_name=bus_axis,
+        split_axis=0,
+        concat_axis=0,
+    ),
+    1,
+)
 
 
 def split_up(array, dim, devices):
@@ -115,7 +124,7 @@
     right_side = gated(normed, w_right, w_right_gate, pair_mask)
     pair_here = exchange_by_chip(pair_rep, (("row_0", "row_1", "row_2"), "row_3"), (1, 0), 1, 0)
     normed_here = normalize(pair_here, in_gain, 2).astype(jnp.bfloat16)
-    triangle = batched_rows(right_side, lax.all_gather(left_side, ROW, axis=1, tiled=True))
+    triangle = batched_rows(right_side, trace_joints(left_side, ROW))
     einsum_form = "kba,kc->abc"
     hidden_total = hid_local * ch_count
     stat_sums = together((jnp.sum(triangle, 0), jnp.sum(triangle * triangle, 0)), "ch")

time: 322 us -> 537 us (1.67); the launches traced: 321 us -> 530 us
  waiting for transfers between devices: 212 us -> 423 us
  between operations: 14.3 us -> 1.18 us
  starting transfers between devices: 24.6 us -> 32.1 us
  local copies, waits for them, and re-layouts: 10.5 us -> 16.6 us
    all_to_all x0 -> x1, waiting for transfers between devices: none -> 414 us  [lax.all_to_all(jnp.stack([block_in] * lax.axis_size(bus_axis)), axis_name...]
    all_gather x1 -> x0, waiting for transfers between devices: 200 us -> none  [local(): lax.all_gather(left_side, ROW, axis=1, tiled=True)]
    all_to_all x0 -> x1, starting transfers between devices: none -> 7.67 us  [lax.all_to_all(jnp.stack([block_in] * lax.axis_size(bus_axis)), axis_name...]
    another operation x0 -> x1, local copies, waits for them, and re-layouts: none -> 7.19 us  [jnp.stack([block_in] * lax.axis_size(bus_axis))]
  transfers between devices with their start and end apart: 4 -> 4, of which waited for: 4 -> 4; matrix products, arithmetic and copies ran while one was open for 4% -> 3% of each run, Pallas kernels for 0% -> 0%
where the time goes in v1:
time: 537 us; the launch traced here: 530 us
  waiting for transfers between devices  423 us (79%)
  matrix products  34.3 us (6%)
  starting transfers between devices  32.1 us (6%)
  local copies, waits for them, and re-layouts  16.6 us (3%)
  blocking collectives  15.6 us (3%)
  other arithmetic  7.43 us (1%)
    all_to_all x1, waiting for transfers between devices, lax.all_to_all(jnp.stack([block_in] * lax.axis_size(bus_axis)), axis_name...  414 us
    dot_general x1, matrix products, batched_rows(): lax.dot_general(first, second, (((2,), (2,)), ((0,), (0,))), preferred_el...  29.3 us
    all_to_all x1, starting transfers between devices, moved_by_axis(): whole = lax.all_to_all(whole, axes[k], k, k, tiled=True)  12.7 us
    psum x1, blocking collectives, packed_total(): so_far = lax.psum(vector, axis)  11.6 us
  transfers between devices with their start and end apart: 4, of which 4 were waited for; matrix products, arithmetic and copies ran while one was open for 3% of the time, Pallas kernels for 0%

profile of v1, /device:TPU:16, one launch (start us, length us, event | category | flops | bytes accessed | tf_op | source)
XLA Modules:
  0.0 530.3 jit_solution(11181164168743135752)
XLA Ops:
  0.6 0.0 copy-start
  0.6 1.3 reshape.156
  2.0 0.1 copy.87
  2.1 4.0 all_to_all.26
  6.0 1.0 copy.88
  7.0 12.7 %all-to-all-start.1 = ((bf16[64,2,3,3,128]{4,1,3,2,0:T(2,128)(2,1)}), bf16[64,2,3,3,128]{4,1,3,2,0:T(2,128)(2,1)S(1)}, u32[]{:S(2)}, u32[]{:S(2)}) async-start(bf16[64,2,3,3,128]{4,1,3,2,0:T(2,128)(2,1)} %copy.88), calls=%async_computation.1 | async-start | bytes 589824 | tf_op jit(solution)/shard_map/all_to_all | solution.py:36
  19.7 1.1 convert_reduce_fusion
  20.8 0.7 convert_element_type.55
  21.5 1.4 fusion.22
  22.9 0.1 dynamic_slice.21
  23.0 0.1 broadcast_multiply_fusion.1
  23.1 1.5 fusion.6
  24.6 1.5 fusion.18
  26.1 7.7 %all-to-all-done.1 = bf16[64,2,3,3,128]{4,1,3,2,0:T(2,128)(2,1)S(1)} async-done(((bf16[64,2,3,3,128]{4,1,3,2,0:T(2,128)(2,1)}), bf16[64,2,3,3,128]{4,1,3,2,0:T(2,128)(2,1)S(1)}, u32[]{:S(2)}, u32[]{:S(2)}) %all-to-all-start.1) | async-done | bytes 294944 | tf_op jit(solution)/shard_map/all_to_all | solution.py:36
  33.8 7.2 %stack.2 = bf16[128,64,3,384]{3,1,2,0:T(8,128)(2,1)} broadcast(bf16[64,3,384]{2,0,1:T(8,128)(2,1)S(1)} %fusion.18), dimensions={1,2,3} | broadcast | bytes 19021824 | tf_op jit(solution)/shard_map/stack | solution.py:11
  41.0 0.0 copy-start.8
  41.0 0.0 copy-start.5
  41.0 7.7 %all-to-all-start.2 = ((bf16[128,64,3,384]{3,1,2,0:T(8,128)(2,1)}), bf16[128,64,3,384]{3,1,2,0:T(8,128)(2,1)}, u32[]{:S(2)}, u32[]{:S(2)}) async-start(bf16[128,64,3,384]{3,1,2,0:T(8,128)(2,1)} %stack.2), calls=%async_computation.2 | async-start | bytes 37748736 | tf_op jit(solution)/shard_map/all_to_all | solution.py:10
  48.7 0.0 copy-start.3
  48.7 0.0 copy-done.6
  48.8 0.1 dynamic_slice.22
  48.8 0.0 copy-done.7
  48.8 0.1 dynamic_slice.23
  48.9 0.0 copy-done.1
  48.9 0.0 copy-done.4
  48.9 0.0 copy-done.8
  48.9 0.5 fusion.9
  49.5 0.0 copy-done.5
  49.5 0.5 fusion.19
  50.0 0.2 copy.89
  50.2 0.2 reshape_reshape.3
  50.4 0.9 convert_reduce_fusion.1
  51.3 0.1 broadcast_multiply_fusion
  51.4 2.0 fusion.26
  53.4 413.8 %all-to-all-done.2 = bf16[128,64,3,384]{3,1,2,0:T(8,128)(2,1)} async-done(((bf16[128,64,3,384]{3,1,2,0:T(8,128)(2,1)}), bf16[128,64,3,384]{3,1,2,0:T(8,128)(2,1)}, u32[]{:S(2)}, u32[]{:S(2)}) %all-to-all-start.2) | async-done | bytes 18874400 | tf_op jit(solution)/shard_map/all_to_all | solution.py:10
  467.2 29.3 %fusion.50 = (f32[3,384]{1,0:T(4,128)S(1)}, f32[3,384]{1,0:T(4,128)S(1)}, f32[64,3,384]{2,1,0:T(4,128)S(1)}) fusion(bf16[64,384,384]{2,0,1:T(8,128)(2,1)} %bitcast.11, bf16[64,3,384]{2,0,1:T(8,128)(2,1)S(1)} %fusion.19), kind=kOutput, calls=%fused_computation.78 | convolution fusion | flops 56841984 | bytes 19325952 | tf_op jit(solution)/shard_map/dot_general | solution.py:94
  496.6 0.8 broadcast_in_dim.2
  497.4 4.8 all-to-all-start.3
  502.2 0.1 constant_dynamic-slice_fusion
  502.3 1.3 copy.92
  503.6 0.2 copy.109
  503.8 0.2 all-to-all-done.3
  504.1 0.1 multiply_convert_fusion.1
  504.3 0.0 copy-done
  504.3 0.3 convolution_convert_fusion
  504.6 0.7 copy.128
  505.3 7.0 %all-to-all-start.4 = ((bf16[2,384,3,64]{1,3,2,0:T(8,128)(2,1)}), bf16[2,384,3,64]{1,3,2,0:T(8,128)(2,1)S(1)}, u32[]{:S(2)}, u32[]{:S(2)}) async-start(bf16[2,384,3,64]{1,3,2,0:T(8,128)(2,1)} %bitcast.42), calls=%async_computation.4 | async-start | bytes 589824 | tf_op jit(solution)/shard_map/all_to_all | solution.py:66
  512.3 0.1 add_rsqrt_fusion
  512.4 1.3 copy.95
  513.7 0.3 rsqrt.26
  513.9 0.3 div.50
  514.2 1.4 all-to-all-done.4
  515.7 0.6 convert_reduce_fusion.3
  516.3 0.0 copy-start.2
  516.3 0.1 copy.102
  516.4 0.2 reshape.163
  516.6 0.1 copy.103
  516.8 0.2 reshape.164
  517.0 11.6 %psum.7 = f32[2304]{0:T(1024)S(1)} all-reduce(f32[2304]{0:T(1024)S(1)} %pad_maximum_fusion.1), channel_id=1, replica_groups=mesh['row_0'=8,'row_1'=2,'row_2'=4,'row_3'=2,'ch'=2] {'ch'}, use_global_device_ids=true, to_apply=%region_10.0 | all-reduce | flops 2304 | bytes 18432 | tf_op jit(solution)/shard_map/psum | solution.py:72
  528.6 0.2 div.64
  528.8 0.1 copy.104
  528.9 0.2 div.66
  529.2 0.1 copy.107
  529.3 0.8 fusion.30
  (20 shorter events, 0.2 us)
Async XLA Ops:
  0.6 503.6 %copy-start = (bf16[128,128]{1,0:T(8,128)(2,1)S(1)}, bf16[128,128]{1,0:T(8,128)(2,1)}, u32[]{:S(2)}) copy-start(bf16[128,128]{1,0:T(8,128)(2,1)} %param.20) | copy-start | bytes 98308
  7.0 26.8 %all-to-all-start.1 = ((bf16[64,2,3,3,128]{4,1,3,2,0:T(2,128)(2,1)}), bf16[64,2,3,3,128]{4,1,3,2,0:T(2,128)(2,1)S(1)}, u32[]{:S(2)}, u32[]{:S(2)}) async-start(bf16[64,2,3,3,128]{4,1,3,2,0:T(2,128)(2,1)} %copy.88), calls=%async_computation.1 | async-start | bytes 589824 | tf_op jit(solution)/shard_map/all_to_all | solution.py:36
  41.0 7.7 %copy-start.6 = (f32[128]{0:T(128)S(1)}, f32[128]{0:T(128)}, u32[]{:S(2)}) copy-start(f32[128]{0:T(128)} %param.19) | copy-start | bytes 1540
  41.0 7.8 %copy-start.7 = (f32[128]{0:T(128)S(1)}, f32[128]{0:T(128)}, u32[]{:S(2)}) copy-start(f32[128]{0:T(128)} %param.21) | copy-start | bytes 1540
  41.0 7.9 %copy-start.1 = (bf16[3,384,128]{2,1,0:T(8,128)(2,1)S(1)}, bf16[3,384,128]{2,1,0:T(8,128)(2,1)}, u32[]{:S(2)}) copy-start(bf16[3,384,128]{2,1,0:T(8,128)(2,1)} %param.11) | copy-start | bytes 884740
  41.0 7.9 %copy-start.4 = (bf16[128,64]{0,1:T(8,128)(2,1)S(1)}, bf16[128,64]{0,1:T(8,128)(2,1)}, u32[]{:S(2)}) copy-start(bf16[128,64]{0,1:T(8,128)(2,1)} %param.17) | copy-start | bytes 49156
  41.0 7.9 %copy-start.8 = (f32[128]{0:T(128)S(1)}, f32[128]{0:T(128)}, u32[]{:S(2)}) copy-start(f32[128]{0:T(128)} %param.13) | copy-start | bytes 1540
  41.0 8.4 %copy-start.5 = (bf16[128,64]{0,1:T(8,128)(2,1)S(1)}, bf16[128,64]{0,1:T(8,128)(2,1)}, u32[]{:S(2)}) copy-start(bf16[128,64]{0,1:T(8,128)(2,1)} %param.16) | copy-start | bytes 49156
  41.0 426.1 %all-to-all-start.2 = ((bf16[128,64,3,384]{3,1,2,0:T(8,128)(2,1)}), bf16[128,64,3,384]{3,1,2,0:T(8,128)(2,1)}, u32[]{:S(2)}, u32[]{:S(2)}) async-start(bf16[128,64,3,384]{3,1,2,0:T(8,128)(2,1)} %stack.2), calls=%async_computation.2 | async-start | bytes 37748736 | tf_op jit(solution)/shard_map/all_to_all | solution.py:10
  48.7 466.9 %copy-start.3 = (bf16[128,128]{1,0:T(8,128)(2,1)S(1)}, bf16[128,128]{1,0:T(8,128)(2,1)}, u32[]{:S(2)}) copy-start(bf16[128,128]{1,0:T(8,128)(2,1)} %param.18) | copy-start | bytes 98308
  497.4 6.6 %all-to-all-start.3 = ((f32[2,1,2304]{2,1,0:T(1,128)}), f32[2,1,2304]{2,1,0:T(1,128)S(1)}, u32[]{:S(2)}, u32[]{:S(2)}) async-start(f32[2,1,2304]{2,1,0:T(1,128)} %broadcast_in_dim.2), calls=%async_computation.3 | async-start | bytes 36864 | tf_op jit(solution)/shard_map/all_to_all | solution.py:48
  505.3 10.3 %all-to-all-start.4 = ((bf16[2,384,3,64]{1,3,2,0:T(8,128)(2,1)}), bf16[2,384,3,64]{1,3,2,0:T(8,128)(2,1)S(1)}, u32[]{:S(2)}, u32[]{:S(2)}) async-start(bf16[2,384,3,64]{1,3,2,0:T(8,128)(2,1)} %bitcast.42), calls=%async_computation.4 | async-start | bytes 589824 | tf_op jit(solution)/shard_map/all_to_all | solution.py:66
  516.3 13.8 %copy-start.2 = (bf16[384,3,64]{0,2,1:T(8,128)(2,1)}, bf16[384,3,64]{0,2,1:T(8,128)(2,1)S(1)}, u32[]{:S(2)}) copy-start(bf16[384,3,64]{0,2,1:T(8,128)(2,1)S(1)} %get-tuple-element.11) | copy-start | bytes 442372
